TPU v7x, 256 devices: a whole 4x4x8 slice. The times are simulated.
256 devices in a mesh: fsdp: 32 (over x_lo, z, core), proto: 4 (over y), dp: 2 (over x_hi).
Axes of the slice: x: 4 (x_hi: 2, x_lo: 2; x = x_hi * 2 + x_lo), y: 4, z: 8, core: 2. Of those that a mesh axis runs over, the one named last changes fastest.
Arguments:
- teacher_weight: float32 [192, 65536], P(None, ('proto', 'fsdp')), may hold values from -0.4375 to 0.4375
- student_weight: float32 [192, 65536], P(None, ('proto', 'fsdp')), may hold values from -0.4375 to 0.4375
- teacher_feats: bfloat16 [2, 8192, 192], P('dp', 'fsdp'), may hold values from -6 to 6
- student_feats: bfloat16 [2, 8192, 192], P('dp', 'fsdp'), may hold values from -6 to 6
- pairing: int32 [2, 8192], P('dp', 'fsdp'), may hold values from 0 to 255
- center: float32 [65536], P('proto'), may hold values from -10.3 to -3.7
Outputs:
- teacher_new: float32 [192, 65536], P(None, ('proto', 'fsdp'))
- student_grad: float32 [192, 65536], P(None, ('proto', 'fsdp', 'dp'))
Inputs may be any that keep to these rules, and one draw needn't show every extreme that they name: pairing[v, r] indexes a crop of the other view in the same block of 256 crops.
All inputs are finite; a program needn't handle non-finite values.
Results may differ from a plain program's by a relative error of at most 0.012.
Values may be sent and summed in bfloat16 or wider, within the bound.
A program may use at most 128 MiB of HBM per device.

v0:
```python
import jax
import jax.numpy as jnp
from jax import lax
from jax.sharding import PartitionSpec as P


def from_partner(shard, axis, apart):
    return lax.ppermute(shard, axis, [(i, i ^ 1 << apart) for i in range(lax.axis_size(axis))])


def normalize_cols(weights):
    return weights * lax.rsqrt(jnp.sum(weights * weights, axis=0, keepdims=True) + 1e-06)


def normalize_rows(feats):
    values = feats.astype(jnp.float32)
    return values * lax.rsqrt(jnp.sum(values * values, axis=-1, keepdims=True) + 1e-06)


def shards(teacher_weight, student_weight, teacher_feats, student_feats, pairing, center):
    teacher_new = 0.994 * teacher_weight + 0.006 * student_weight
    w_teacher = normalize_cols(teacher_new).astype(jnp.bfloat16)
    w_student = normalize_cols(student_weight).astype(jnp.bfloat16)
    z_teacher = normalize_rows(teacher_feats[0]).astype(jnp.bfloat16)
    z_student = normalize_rows(student_feats[0]).astype(jnp.bfloat16)
    swapped = from_partner(z_teacher, "dp", 0)
    paired = jnp.take(swapped, pairing[0], axis=0)
    logits_t = jnp.dot(
        paired,
        lax.all_gather(w_teacher, "fsdp", axis=1, tiled=True),
        preferred_element_type=jnp.float32,
    )
    logits_s = jnp.dot(
        z_student,
        lax.all_gather(w_student, "fsdp", axis=1, tiled=True),
        preferred_element_type=jnp.float32,
    )
    scores_t = (logits_t - center[None, :]) / 0.04
    scores_s = logits_s / 0.1
    local_max_t = jnp.max(scores_t, axis=1)
    local_max_s = jnp.max(scores_s, axis=1)
    max_t, max_s = lax.pmax((local_max_t, local_max_s), "proto")
    exp_t = jnp.exp(scores_t - max_t[:, None])
    exp_s = jnp.exp(scores_s - max_s[:, None])
    total_t, total_s = lax.psum((jnp.sum(exp_t, axis=1), jnp.sum(exp_s, axis=1)), "proto")
    derivs = ((exp_s / total_s[:, None] - exp_t / total_t[:, None]) / 0.1).astype(jnp.bfloat16)
    grad_rows_mine = lax.psum_scatter(
        lax.dot_general(
            derivs, z_student, (((0,), (0,)), ((), ())), preferred_element_type=jnp.float32
        ),
        ("fsdp", "dp"),
        scatter_dimension=0,
        tiled=True,
    )
    grad_part = grad_rows_mine.T
    width = grad_part.shape[1]
    offset = lax.axis_index("dp") * width
    student_part = lax.dynamic_slice_in_dim(student_weight, offset, width, 1)
    norms = jnp.sqrt(jnp.sum(student_part * student_part, axis=0, keepdims=True) + 1e-06)
    unit = student_part / norms
    student_grad = (grad_part - unit * jnp.sum(unit * grad_part, axis=0, keepdims=True)) / norms
    return (teacher_new, student_grad)


def solution(mesh):
    placed = (
        P(None, ("proto", "fsdp")),
        P(None, ("proto", "fsdp")),
        P("dp", "fsdp", None),
        P("dp", "fsdp", None),
        P("dp", "fsdp"),
        P("proto"),
    )
    return jax.shard_map(
        shards,
        mesh=mesh,
        in_specs=placed,
        out_specs=(P(None, ("proto", "fsdp")), P(None, ("proto", "fsdp", "dp"))),
        check_vma=False,
    )
```

profile of v0, /device:TPU:8, one launch (start us, length us, event | category | flops | bytes accessed | tf_op | source)
XLA Modules:
  0.0 518.9 jit_solution(17187875234807501835)
XLA Ops:
  7.2 0.0 copy-start.3
  7.2 0.0 all-gather.3.cloned.1.call-start
  7.2 1.0 multiply_reduce_fusion.1
  8.3 1.9 multiply_reduce_fusion
  10.2 0.0 all-gather.3.cloned.1.call-update
  10.2 0.0 all-gather.5.cloned.1.call-start
  10.3 0.7 multiply_convert_fusion.2
  11.0 0.0 all-gather.5.cloned.1.call-update
  11.0 0.0 reduce-scatter.2.cloned.1.call-start
  11.0 1.0 copy.9
  12.0 0.1 fusion.4
  12.2 0.1 fusion.5
  12.3 3.1 collective-permute-start
  15.4 0.9 fusion.6
  16.3 0.7 compare_and_fusion
  17.0 0.7 compare_select_fusion
  17.7 1.4 collective-permute-done
  19.1 1.2 gather_fusion
  20.3 63.3 %all-gather.3.cloned.1.call-done = bf16[192,16384]{1,0:T(8,128)(2,1)} async-done(((bf16[192,512]{1,0:T(8,128)(2,1)}), bf16[192,16384]{1,0:T(8,128)(2,1)}) %all-gather.3.cloned.1.call-update) | async-done | bytes 6291472 | tf_op jit(solution)/shard_map/all_gather | solution.py:35
  83.6 11.0 %fusion.18 = (f32[256]{0:T(256)S(1)}, f32[256,16384]{1,0:T(8,128)}) fusion(bf16[192,16384]{1,0:T(8,128)(2,1)} %all-gather.3.cloned.1.call-done, bf16[1,256,192]{1,2,0:T(8,128)(2,1)} %param.9, f32[256]{0:T(256)S(1)} %add_rsqrt_fusion.3), kind=kOutput, calls=%fused_computation.44 | convolution fusion | flops 1619148544 | bytes 23169024 | tf_op jit(solution)/shard_map/dot_general | solution.py:33
  94.6 61.0 %all-gather.5.cloned.1.call-done = bf16[192,16384]{1,0:T(8,128)(2,1)} async-done(((bf16[192,512]{1,0:T(8,128)(2,1)}), bf16[192,16384]{1,0:T(8,128)(2,1)}) %all-gather.5.cloned.1.call-update) | async-done | bytes 6291472 | tf_op jit(solution)/shard_map/all_gather | solution.py:30
  155.6 0.0 copy-done.3
  155.6 10.0 %fusion.17 = (f32[256]{0:T(256)S(1)}, f32[256,16384]{1,0:T(8,128)}) fusion(f32[16384]{0:T(1024)S(1)} %copy-done.3, bf16[192,16384]{1,0:T(8,128)(2,1)} %all-gather.5.cloned.1.call-done, bf16[256,192]{1,0:T(8,128)(2,1)S(1)} %gather_fusion, pred[256]{0:T(512)(128)(4,1)S(1)} %compare_and_fusion), kind=kOutput, calls=%fused_computation.43 | convolution fusion | flops 1623244544 | bytes 23233792 | tf_op jit(solution)/shard_map/dot_general | solution.py:28
  165.6 0.0 copy-done.1
  165.6 8.6 %all-reduce.1 = (f32[256]{0:T(256)S(1)}, f32[256]{0:T(256)S(1)}) all-reduce(f32[256]{0:T(256)S(1)} %get-tuple-element.9, f32[256]{0:T(256)S(1)} %get-tuple-element.11), channel_id=1, replica_groups=mesh['fsdp'=32,'proto'=4,'dp'=2] {'proto'}, use_global_device_ids=true, to_apply=%region_9.10 | all-reduce | flops 512 | bytes 4096 | tf_op jit(solution)/shard_map/pmax | solution.py:42
  174.2 12.2 %fusion.1 = (f32[256]{0:T(256)S(1)}, f32[256]{0:T(256)S(1)}) fusion(f32[256,16384]{1,0:T(8,128)} %get-tuple-element.12, f32[256]{0:T(256)S(1)} %get-tuple-element.5, f32[256,16384]{1,0:T(8,128)} %get-tuple-element.10, f32[256]{0:T(256)S(1)} %get-tuple-element.4), kind=kLoop, calls=%fused_computation.7 | loop fusion | flops 16776704 | bytes 33558528 | tf_op jit(solution)/shard_map/reduce_sum | solution.py:45
  186.3 10.1 %all-reduce = (f32[256]{0:T(256)S(1)}, f32[256]{0:T(256)S(1)}) all-reduce(f32[256]{0:T(256)S(1)} %get-tuple-element.14, f32[256]{0:T(256)S(1)} %get-tuple-element.13), channel_id=1, replica_groups=mesh['fsdp'=32,'proto'=4,'dp'=2] {'proto'}, use_global_device_ids=true, to_apply=%region_11.12 | all-reduce | flops 512 | bytes 4096 | tf_op jit(solution)/shard_map/psum | solution.py:45
  196.5 17.4 %fusion.3 = f32[16384,192]{0,1:T(8,128)} fusion(f32[256,16384]{1,0:T(8,128)} %get-tuple-element.12, f32[256,16384]{1,0:T(8,128)} %get-tuple-element.10, f32[256]{0:T(256)S(1)} %get-tuple-element.2, f32[256]{0:T(256)S(1)} %get-tuple-element.4, f32[256]{0:T(256)S(1)} %get-tuple-element.3, f32[256]{0:T(256)S(1)} %get-tuple-element.5, ...), kind=kOutput, calls=%fused_computation.9 | convolution fusion | flops 1640120320 | bytes 46240768 | tf_op jit(solution)/shard_map/dot_general | solution.py:48
  213.9 0.0 reduce-scatter.2.cloned.1.call-update
  214.0 295.8 %reduce-scatter.2.cloned.1.call-done = f32[256,192]{0,1:T(8,128)} async-done(((f32[16384,192]{0,1:T(8,128)}), f32[256,192]{0,1:T(8,128)}) %reduce-scatter.2.cloned.1.call-update) | async-done | bytes 196624 | tf_op jit(solution)/shard_map/reduce_scatter | solution.py:47
  509.8 1.0 fusion.8
  510.7 1.6 fusion.9
  (12 shorter events, 0.1 us)
Async XLA Ops:
  7.2 148.4 %copy-start.3 = (f32[16384]{0:T(1024)S(1)}, f32[16384]{0:T(1024)}, u32[]{:S(2)}) copy-start(f32[16384]{0:T(1024)} %param.11) | copy-start | bytes 196612
  7.2 76.4 %all-gather.3.cloned.1.call-start = ((), (), s32[]{:S(2)}) async-start(), calls=%async_computation.1 | async-start | bytes 6488064 | tf_op jit(solution)/shard_map/all_gather | solution.py:35
  10.2 155.4 %copy-start.1 = (f32[192,512]{1,0:T(8,128)}, f32[192,512]{1,0:T(8,128)S(1)}, u32[]{:S(2)}) copy-start(f32[192,512]{1,0:T(8,128)S(1)} %get-tuple-element.7) | copy-start | bytes 1179652
  10.2 145.4 %all-gather.5.cloned.1.call-start = ((), (), s32[]{:S(2)}) async-start(), calls=%async_computation.2 | async-start | bytes 6488064 | tf_op jit(solution)/shard_map/all_gather | solution.py:30
  11.0 498.8 %reduce-scatter.2.cloned.1.call-start = ((), (), s32[]{:S(2)}) async-start(), calls=%async_computation.3 | async-start | bytes 12779520 | tf_op jit(solution)/shard_map/reduce_scatter | solution.py:47
  12.3 6.8 %collective-permute-start = (bf16[256,192]{1,0:T(8,128)(2,1)S(1)}, bf16[256,192]{1,0:T(8,128)(2,1)S(1)}, u32[]{:S(2)}, u32[]{:S(2)}) collective-permute-start(bf16[256,192]{1,0:T(8,128)(2,1)S(1)} %fusion.5), channel_id=1, source_target_pairs={{0,1},{1,0},{2,3},{3,2},{4,5},{5,4},{6,7},{7,6},{8,9},{9,8},{10,11... | collective-permute-start | bytes 294920 | tf_op jit(solution)/shard_map/ppermute | solution.py:8
  174.2 22.3 %copy-start.2 = (bf16[1,256,192]{1,2,0:T(8,128)(2,1)S(1)}, bf16[1,256,192]{1,2,0:T(8,128)(2,1)}, u32[]{:S(2)}) copy-start(bf16[1,256,192]{1,2,0:T(8,128)(2,1)} %param.9) | copy-start | bytes 294916
  196.5 17.5 %copy-start = (f32[192,512]{1,0:T(8,128)S(1)}, f32[192,512]{1,0:T(8,128)}, u32[]{:S(2)}) copy-start(f32[192,512]{1,0:T(8,128)} %param.7) | copy-start | bytes 1179652
Sparse Core Ops, SparseCore 0:
  10.5 73.0 all-gather.2
  85.4 70.0 all-gather.4
  214.0 295.6 reduce-scatter.1
where the time goes:
time: 519 us
  waiting for transfers between devices  422 us (81%)
  matrix products  38.4 us (7%)
  other arithmetic  21 us (4%)
  blocking collectives  18.7 us (4%)
  between operations  13.8 us (3%)
    reduce_scatter x1, waiting for transfers between devices, shards(): lax.psum_scatter(lax.dot_general(derivs, z_student, (((0,), (0,)), ((), (...  296 us
    all_gather x1, waiting for transfers between devices, shards(): lax.all_gather(w_student, 'fsdp', axis=1, tiled=True)  63.3 us
    all_gather x1, waiting for transfers between devices, shards(): lax.all_gather(w_teacher, 'fsdp', axis=1, tiled=True)  61 us
    dot_general x1, matrix products, shards(): lax.dot_general(derivs, z_student, (((0,), (0,)), ((), ())), preferred_el...  17.4 us
    reduce_sum x1, other arithmetic, shards(): jnp.sum(exp_s, axis=1)  12.2 us
    dot_general x1, matrix products, shards(): jnp.dot(z_student, lax.all_gather(w_student, 'fsdp', axis=1, tiled=True),...  11 us
  transfers between devices with their start and end apart: 4, of which 4 were waited for; matrix products, arithmetic and copies ran while one was open for 3% of the time, Pallas kernels for 0%

commit v1 on v0

--- a/solution.py
+++ b/solution.py
@@ -27,7 +27,9 @@
     paired = jnp.take(swapped, pairing[0], axis=0)
     logits_t = jnp.dot(
         paired,
-        lax.all_gather(w_teacher, "fsdp", axis=1, tiled=True),
+        jnp.concatenate(
+            lax.all_to_all(jnp.stack([w_teacher] * lax.axis_size("fsdp")), "fsdp", 0, 0), axis=1
+        ),
         preferred_element_type=jnp.float32,
     )
     logits_s = jnp.dot(

time: 519 us -> 573 us (1.10)
  waiting for transfers between devices: 422 us -> 465 us
  starting transfers between devices: 3.23 us -> 12.8 us
  local copies, waits for them, and re-layouts: 2.16 us -> 8.2 us
    all_to_all x0 -> x1, waiting for transfers between devices: none -> 151 us  [shards(): lax.all_to_all(jnp.stack([w_teacher] * lax.axis_size('fsdp')), 'fsdp', 0, 0)]
    all_gather x1, waiting for transfers between devices: 63.3 us -> 0.01 us  [shards(): lax.all_gather(w_student, 'fsdp', axis=1, tiled=True)]
    all_gather x1 -> x0, waiting for transfers between devices: 61 us -> none  [shards(): lax.all_gather(w_teacher, 'fsdp', axis=1, tiled=True)]
    ppermute x1, waiting for transfers between devices: 1.4 us -> 15.7 us  [from_partner(): lax.ppermute(shard, axis, [(i, i ^ 1 << apart) for i in range(lax.axis_si...]
    all_to_all x0 -> x1, starting transfers between devices: none -> 9.9 us  [shards(): lax.all_to_all(jnp.stack([w_teacher] * lax.axis_size('fsdp')), 'fsdp', 0, 0)]
  transfers between devices with their start and end apart: 4 -> 4, of which waited for: 4 -> 3; matrix products, arithmetic and copies ran while one was open for 3% -> 2% of each run, Pallas kernels for 0% -> 0%
where the time goes in v1:
time: 573 us
  waiting for transfers between devices  465 us (81%)
  matrix products  35.7 us (6%)
  blocking collectives  19.2 us (3%)
  other arithmetic  18.1 us (3%)
  between operations  14.2 us (2%)
  starting transfers between devices  12.8 us (2%)
  local copies, waits for them, and re-layouts  8.2 us (1%)
    reduce_scatter x1, waiting for transfers between devices, shards(): lax.psum_scatter(lax.dot_general(derivs, z_student, (((0,), (0,)), ((), (...  298 us
    all_to_all x1, waiting for transfers between devices, shards(): lax.all_to_all(jnp.stack([w_teacher] * lax.axis_size('fsdp')), 'fsdp', 0, 0)  151 us
    dot_general x1, matrix products, shards(): lax.dot_general(derivs, z_student, (((0,), (0,)), ((), ())), preferred_el...  17.4 us
    ppermute x1, waiting for transfers between devices, from_partner(): lax.ppermute(shard, axis, [(i, i ^ 1 << apart) for i in range(lax.axis_si...  15.7 us
    reduce_sum x1, other arithmetic, shards(): jnp.sum(exp_s, axis=1)  12.1 us
  transfers between devices with their start and end apart: 4, of which 3 were waited for; matrix products, arithmetic and copies ran while one was open for 2% of the time, Pallas kernels for 0%

profile of v1, /device:TPU:8, one launch (start us, length us, event | category | flops | bytes accessed | tf_op | source)
XLA Modules:
  0.0 573.0 jit_solution(16989823703506293173)
XLA Ops:
  7.2 0.0 copy-start.4
  7.2 0.0 copy-start.2
  7.2 0.0 copy-start.5
  7.2 1.1 multiply_reduce_fusion.1
  8.3 1.9 multiply_reduce_fusion
  10.2 0.0 copy-start.3
  10.2 3.4 stack.2
  13.6 9.9 %all-to-all-start = ((bf16[32,192,512]{2,1,0:T(8,128)(2,1)}), bf16[32,192,512]{2,1,0:T(8,128)(2,1)}, u32[]{:S(2)}, u32[]{:S(2)}) async-start(bf16[32,192,512]{2,1,0:T(8,128)(2,1)} %stack.2), calls=%async_computation | async-start | bytes 12582912 | tf_op jit(solution)/shard_map/all_to_all | solution.py:31
  23.5 0.0 all-gather.2.cloned.1.call-start
  23.6 0.7 all-gather.2.cloned.1.call-update
  24.3 0.0 reduce-scatter.2.cloned.1.call-start
  24.3 0.0 copy-done.4
  24.3 0.1 copy.10
  24.4 0.1 fusion.4
  24.5 0.1 fusion.5
  24.7 2.8 collective-permute-start
  27.5 0.0 copy-done.2
  27.5 0.0 copy-done.5
  27.6 15.7 %collective-permute-done = bf16[256,192]{1,0:T(8,128)(2,1)S(1)} collective-permute-done((bf16[256,192]{1,0:T(8,128)(2,1)S(1)}, bf16[256,192]{1,0:T(8,128)(2,1)S(1)}, u32[]{:S(2)}, u32[]{:S(2)}) %collective-permute-start) | collective-permute-done | bytes 98336 | tf_op jit(solution)/shard_map/ppermute | solution.py:8
  43.2 1.2 gather_fusion
  44.4 150.8 %all-to-all-done = bf16[32,192,512]{2,1,0:T(8,128)(2,1)} async-done(((bf16[32,192,512]{2,1,0:T(8,128)(2,1)}), bf16[32,192,512]{2,1,0:T(8,128)(2,1)}, u32[]{:S(2)}, u32[]{:S(2)}) %all-to-all-start) | async-done | bytes 6291488 | tf_op jit(solution)/shard_map/all_to_all | solution.py:31
  195.2 3.6 copy.12
  198.8 7.3 %fusion.17 = (f32[256]{0:T(256)S(1)}, f32[256,16384]{1,0:T(8,128)}) fusion(f32[16384]{0:T(1024)S(1)} %copy-done.3, bf16[192,16384]{1,0:T(8,128)(2,1)S(1)} %bitcast.28, bf16[256,192]{1,0:T(8,128)(2,1)S(1)} %gather_fusion, pred[256]{0:T(512)(128)(4,1)S(1)} %compare_and_fusion), kind=kOutput, calls=%fused_computation.43 | convolution fusion | flops 1623244544 | bytes 23233792 | tf_op jit(solution)/shard_map/dot_general | solution.py:28
  206.1 10.9 %fusion.18 = (f32[256]{0:T(256)S(1)}, f32[256,16384]{1,0:T(8,128)}) fusion(bf16[192,16384]{1,0:T(8,128)(2,1)} %all-gather.2.cloned.1.call-done, bf16[1,256,192]{1,2,0:T(8,128)(2,1)S(1)} %copy-done.2, f32[256]{0:T(256)S(1)} %add_rsqrt_fusion.3), kind=kOutput, calls=%fused_computation.44 | convolution fusion | flops 1619148544 | bytes 23169024 | tf_op jit(solution)/shard_map/dot_general | solution.py:35
  217.1 8.6 %all-reduce.1 = (f32[256]{0:T(256)S(1)}, f32[256]{0:T(256)S(1)}) all-reduce(f32[256]{0:T(256)S(1)} %get-tuple-element.9, f32[256]{0:T(256)S(1)} %get-tuple-element.11), channel_id=1, replica_groups=mesh['fsdp'=32,'proto'=4,'dp'=2] {'proto'}, use_global_device_ids=true, to_apply=%region_9.10 | all-reduce | flops 512 | bytes 4096 | tf_op jit(solution)/shard_map/pmax | solution.py:44
  225.7 12.1 %fusion.1 = (f32[256]{0:T(256)S(1)}, f32[256]{0:T(256)S(1)}) fusion(f32[256,16384]{1,0:T(8,128)} %get-tuple-element.12, f32[256]{0:T(256)S(1)} %get-tuple-element.5, f32[256,16384]{1,0:T(8,128)} %get-tuple-element.10, f32[256]{0:T(256)S(1)} %get-tuple-element.4), kind=kLoop, calls=%fused_computation.7 | loop fusion | flops 16776704 | bytes 33558528 | tf_op jit(solution)/shard_map/reduce_sum | solution.py:47
  237.8 10.5 %all-reduce = (f32[256]{0:T(256)S(1)}, f32[256]{0:T(256)S(1)}) all-reduce(f32[256]{0:T(256)S(1)} %get-tuple-element.14, f32[256]{0:T(256)S(1)} %get-tuple-element.13), channel_id=1, replica_groups=mesh['fsdp'=32,'proto'=4,'dp'=2] {'proto'}, use_global_device_ids=true, to_apply=%region_11.12 | all-reduce | flops 512 | bytes 4096 | tf_op jit(solution)/shard_map/psum | solution.py:47
  248.4 17.4 %fusion.3 = f32[16384,192]{0,1:T(8,128)} fusion(f32[256,16384]{1,0:T(8,128)} %get-tuple-element.12, f32[256,16384]{1,0:T(8,128)} %get-tuple-element.10, f32[256]{0:T(256)S(1)} %get-tuple-element.2, f32[256]{0:T(256)S(1)} %get-tuple-element.4, f32[256]{0:T(256)S(1)} %get-tuple-element.3, f32[256]{0:T(256)S(1)} %get-tuple-element.5, ...), kind=kOutput, calls=%fused_computation.9 | convolution fusion | flops 1640120320 | bytes 46240768 | tf_op jit(solution)/shard_map/dot_general | solution.py:50
  265.8 0.0 reduce-scatter.2.cloned.1.call-update
  265.9 297.6 %reduce-scatter.2.cloned.1.call-done = f32[256,192]{0,1:T(8,128)} async-done(((f32[16384,192]{0,1:T(8,128)}), f32[256,192]{0,1:T(8,128)}) %reduce-scatter.2.cloned.1.call-update) | async-done | bytes 196624 | tf_op jit(solution)/shard_map/reduce_scatter | solution.py:49
  563.5 1.0 fusion.8
  564.5 1.6 fusion.9
  (17 shorter events, 0.2 us)
Async XLA Ops:
  7.2 17.1 %copy-start.4 = (bf16[1,256,192]{1,2,0:T(8,128)(2,1)S(1)}, bf16[1,256,192]{1,2,0:T(8,128)(2,1)}, u32[]{:S(2)}) copy-start(bf16[1,256,192]{1,2,0:T(8,128)(2,1)} %param.8) | copy-start | bytes 294916
  7.2 20.3 %copy-start.2 = (bf16[1,256,192]{1,2,0:T(8,128)(2,1)S(1)}, bf16[1,256,192]{1,2,0:T(8,128)(2,1)}, u32[]{:S(2)}) copy-start(bf16[1,256,192]{1,2,0:T(8,128)(2,1)} %param.9) | copy-start | bytes 294916
  7.2 20.3 %copy-start.5 = (s32[1,256]{1,0:T(1,128)S(1)}, s32[1,256]{1,0:T(1,128)}, u32[]{:S(2)}) copy-start(s32[1,256]{1,0:T(1,128)} %param.10) | copy-start | bytes 3076
  10.2 188.6 %copy-start.1 = (f32[192,512]{1,0:T(8,128)}, f32[192,512]{1,0:T(8,128)S(1)}, u32[]{:S(2)}) copy-start(f32[192,512]{1,0:T(8,128)S(1)} %get-tuple-element.7) | copy-start | bytes 1179652
  10.2 188.5 %copy-start.3 = (f32[16384]{0:T(1024)S(1)}, f32[16384]{0:T(1024)}, u32[]{:S(2)}) copy-start(f32[16384]{0:T(1024)} %param.11) | copy-start | bytes 196612
  13.6 181.6 %all-to-all-start = ((bf16[32,192,512]{2,1,0:T(8,128)(2,1)}), bf16[32,192,512]{2,1,0:T(8,128)(2,1)}, u32[]{:S(2)}, u32[]{:S(2)}) async-start(bf16[32,192,512]{2,1,0:T(8,128)(2,1)} %stack.2), calls=%async_computation | async-start | bytes 12582912 | tf_op jit(solution)/shard_map/all_to_all | solution.py:31
  23.5 182.6 %all-gather.2.cloned.1.call-start = ((), (), s32[]{:S(2)}) async-start(), calls=%async_computation.2 | async-start | bytes 6488064 | tf_op jit(solution)/shard_map/all_gather | solution.py:37
  24.3 539.2 %reduce-scatter.2.cloned.1.call-start = ((), (), s32[]{:S(2)}) async-start(), calls=%async_computation.3 | async-start | bytes 12779520 | tf_op jit(solution)/shard_map/reduce_scatter | solution.py:49
  24.7 18.6 %collective-permute-start = (bf16[256,192]{1,0:T(8,128)(2,1)S(1)}, bf16[256,192]{1,0:T(8,128)(2,1)S(1)}, u32[]{:S(2)}, u32[]{:S(2)}) collective-permute-start(bf16[256,192]{1,0:T(8,128)(2,1)S(1)} %fusion.5), channel_id=1, source_target_pairs={{0,1},{1,0},{2,3},{3,2},{4,5},{5,4},{6,7},{7,6},{8,9},{9,8},{10,11... | collective-permute-start | bytes 294920 | tf_op jit(solution)/shard_map/ppermute | solution.py:8
  248.4 17.5 %copy-start = (f32[192,512]{1,0:T(8,128)S(1)}, f32[192,512]{1,0:T(8,128)}, u32[]{:S(2)}) copy-start(f32[192,512]{1,0:T(8,128)} %param.7) | copy-start | bytes 1179652
Sparse Core Ops, SparseCore 0:
  26.8 141.6 all-gather.1
  265.9 297.5 reduce-scatter.1
